TPU v7x, 256 devices: a whole 4x4x8 slice. The times are simulated.
256 devices in a mesh: dp: 32 (over x, z), expert: 8 (over y, core).
Axes of the slice: x: 4, y: 4, z: 8, core: 2. Of those that a mesh axis runs over, the one named last changes fastest.
Arguments:
- text_embed: bfloat16 [16384, 2048], P(('dp', 'expert')), may hold values from -6 to 6
- image_feats: bfloat16 [8192, 4608], P(('dp', 'expert')), may hold values from -6 to 6
- tile_pos: int32 [8192], P(('dp', 'expert')), may hold values from 0 to 16383, as said below
- proj_in: bfloat16 [4608, 2048], P(None, 'expert'), may hold values from -0.09375 to 0.09375
- proj_out: bfloat16 [2048, 2048], P('expert'), may hold values from -0.125 to 0.125
- norm_gain: float32 [2048], replicated, may hold values from 0.1 to 1.9
- shared_gate: bfloat16 [2048, 2816], P(None, 'expert'), may hold values from -0.125 to 0.125
- shared_up: bfloat16 [2048, 2816], P(None, 'expert'), may hold values from -0.125 to 0.125
- shared_down: bfloat16 [2816, 2048], P('expert'), may hold values from -0.109375 to 0.109375
- expert_gate: bfloat16 [32, 2048, 1408], P('dp', None, 'expert'), may hold values from -0.125 to 0.125
- expert_up: bfloat16 [32, 2048, 1408], P('dp', None, 'expert'), may hold values from -0.125 to 0.125
- expert_down: bfloat16 [32, 1408, 2048], P('dp', 'expert'), may hold values from -0.15625 to 0.15625
- route_ids: int32 [16384, 2], P(('dp', 'expert')), may hold values from 0 to 31, all different within a row; in each aligned block of 512 rows (0 to 511, 512 to 1023, ...) at most 48 rows name the same one
- route_wts: int32 [16384, 2], P(('dp', 'expert')), may hold values from 1 to 65535
Outputs:
- block_out: bfloat16 [16384, 2048], P(('dp', 'expert'))
Inputs may be any that keep to these rules, and one draw needn't show every extreme that they name: `tile_pos`: positions are distinct. The 32 image tokens of one device go 1 to each index of dp, always to rows held by the devices with the sender's own index of expert. `route_ids`: in each aligned block of 512 rows no expert is named by more than 48 rows, a bound that some block reaches.
All inputs are finite; a program needn't handle non-finite values.
Results may differ from a plain program's by a relative error of at most 0.018.
Values may be sent and summed in bfloat16 or wider, within the bound.
A program may use at most 128 MiB of HBM per device.

v0:
```python
import jax
import jax.numpy as jnp
from jax import lax
from jax.sharding import PartitionSpec as P


def normalize(rows, norm_gain):
    rows_f = rows.astype(jnp.float32)
    meansq = jnp.mean(rows_f * rows_f, axis=-1, keepdims=True) + 1e-06
    return (rows_f * lax.rsqrt(meansq) * norm_gain).astype(jnp.bfloat16)


def project_part(feats, proj_in, proj_out):
    vis_hidden = jax.nn.gelu(
        jnp.dot(feats, proj_in, preferred_element_type=jnp.float32), approximate=True
    ).astype(jnp.bfloat16)
    return jnp.dot(vis_hidden, proj_out, preferred_element_type=jnp.float32)


def shards(
    text_embed,
    image_feats,
    tile_pos,
    proj_in,
    proj_out,
    norm_gain,
    shared_gate,
    shared_up,
    shared_down,
    expert_gate,
    expert_up,
    expert_down,
    route_ids,
    route_wts,
):
    tok_dev = text_embed.shape[0]
    img_dev = image_feats.shape[0]
    width_model = text_embed.shape[1]
    n_data = lax.axis_size("dp")
    n_group = lax.axis_size("expert")
    peer = img_dev // n_data
    my_place = lax.axis_index("expert")
    owner = tile_pos // tok_dev
    dest_index = owner // n_group
    order = jnp.argsort(dest_index, stable=True)
    sorted_feats = image_feats[order].reshape(n_data, peer, image_feats.shape[1])
    sorted_offs = (tile_pos[order] % tok_dev).reshape(n_data, peer)
    moved_feats, moved_offs = (
        lax.all_to_all(sorted_feats, "dp", split_axis=0, concat_axis=0, tiled=True),
        lax.all_to_all(sorted_offs, "dp", split_axis=0, concat_axis=0, tiled=True),
    )
    moved_feats = moved_feats.reshape(img_dev, image_feats.shape[1])
    moved_offs = moved_offs.reshape(img_dev)
    texts, feats, offsets, ids, weights = (
        lax.all_gather(text_embed, "expert", axis=0, tiled=True),
        lax.all_gather(moved_feats, "expert", axis=0, tiled=True),
        lax.all_gather(moved_offs, "expert", axis=0, tiled=True),
        lax.all_gather(route_ids, "expert", axis=0, tiled=True),
        lax.all_gather(route_wts, "expert", axis=0, tiled=True),
    )
    partial_value = project_part(feats, proj_in, proj_out)
    projected = lax.psum(partial_value.astype(jnp.bfloat16), "expert")
    block_start = jnp.arange(offsets.shape[0], dtype=jnp.int32) // img_dev * tok_dev
    embed_group = texts.at[offsets + block_start].set(projected)
    normed = normalize(embed_group, norm_gain)
    own_rows = lax.dynamic_slice_in_dim(embed_group, my_place * tok_dev, tok_dev, 0)
    gate_s = jnp.dot(normed, shared_gate, preferred_element_type=jnp.float32)
    up_s = jnp.dot(normed, shared_up, preferred_element_type=jnp.float32)
    shared_hidden = (jax.nn.silu(gate_s) * up_s).astype(jnp.bfloat16)
    group_rows = normed.shape[0]
    top_count = ids.shape[1]
    capacity = 3 * group_rows * top_count // (2 * n_data)
    share = capacity // n_group
    flat_ids = ids.reshape(-1)
    onehot = (flat_ids[:, None] == jnp.arange(n_data, dtype=jnp.int32)[None, :]).astype(jnp.int32)
    rank = jnp.sum(jnp.cumsum(onehot, axis=0) * onehot, axis=1) - 1
    pair_token = jnp.arange(group_rows * top_count, dtype=jnp.int32) // top_count
    send = (
        jnp.zeros((n_data, capacity, width_model), jnp.bfloat16)
        .at[flat_ids, rank]
        .set(normed[pair_token])
    )
    slots = lax.all_to_all(send, "dp", split_axis=0, concat_axis=0, tiled=True)
    gate_e = jnp.einsum("ncd,df->ncf", slots, expert_gate[0], preferred_element_type=jnp.float32)
    up_e = jnp.einsum("ncd,df->ncf", slots, expert_up[0], preferred_element_type=jnp.float32)
    hidden_e = (jax.nn.silu(gate_e) * up_e).astype(jnp.bfloat16)
    partial_out = jnp.einsum(
        "ncf,fd->ncd", hidden_e, expert_down[0], preferred_element_type=jnp.float32
    )
    summed = lax.psum_scatter(
        partial_out.astype(jnp.bfloat16), "expert", scatter_dimension=1, tiled=True
    )
    returned = lax.all_to_all(summed, "dp", split_axis=0, concat_axis=0, tiled=True)
    inside = rank // share == my_place
    local_slot = jnp.where(inside, rank - my_place * share, 0)
    picked = returned.reshape(n_data * share, width_model)[flat_ids * share + local_slot]
    weights_f = weights.astype(jnp.float32)
    weights_n = weights_f / jnp.sum(weights_f, axis=1, keepdims=True)
    coef = jnp.where(inside, weights_n.reshape(-1), 0.0)
    combined = jnp.sum(
        (picked.astype(jnp.float32) * coef[:, None]).reshape(group_rows, top_count, width_model),
        axis=1,
    )
    total = lax.psum_scatter(
        (jnp.dot(shared_hidden, shared_down, preferred_element_type=jnp.float32) + combined).astype(
            jnp.bfloat16
        ),
        "expert",
        scatter_dimension=0,
        tiled=True,
    ).astype(jnp.float32)
    return (own_rows.astype(jnp.float32) + total).astype(jnp.bfloat16)


def solution(mesh):
    return jax.shard_map(
        shards,
        mesh=mesh,
        in_specs=(
            P(("dp", "expert"), None),
            P(("dp", "expert"), None),
            P(("dp", "expert")),
            P(None, "expert"),
            P("expert", None),
            P(),
            P(None, "expert"),
            P(None, "expert"),
            P("expert", None),
            P("dp", None, "expert"),
            P("dp", None, "expert"),
            P("dp", "expert", None),
            P(("dp", "expert"), None),
            P(("dp", "expert"), None),
        ),
        out_specs=P(("dp", "expert"), None),
        check_vma=False,
    )
```

profile of v0, /device:TPU:2, one launch (start us, length us, event | category | flops | bytes accessed | tf_op | source)
XLA Modules:
  0.0 534.1 jit_solution(12676066431425173796)
XLA Ops:
  6.5 0.8 and_select_fusion.4
  7.4 1.6 sort.17
  9.0 2.0 gather_fusion.1
  11.0 0.5 broadcast.394
  11.5 0.8 reduce.7
  12.4 23.1 %all_to_all.21 = bf16[32,2,2304]{2,1,0:T(2,128)(2,1)S(1)} all-to-all(bf16[32,2,2304]{2,1,0:T(2,128)(2,1)S(1)} %reshape.350), channel_id=1, replica_groups=mesh['dp'=32,'expert'=8] {'dp'}, dimensions={0} | all-to-all | bytes 589824 | tf_op jit(solution)/shard_map/all_to_all | solution.py:49
  35.6 0.2 reshape.351
  35.9 0.8 copy.50
  36.7 0.7 all-gather.7.cloned.1.call-update
  37.4 0.7 gather_fusion
  38.1 0.7 copy.48
  38.8 5.8 %all-to-all-start = ((s32[32,1,1]{2,1,0:T(1,128)}), s32[32,1,1]{2,1,0:T(1,128)S(1)}, u32[]{:S(2)}, u32[]{:S(2)}) async-start(s32[32,1,1]{2,1,0:T(1,128)} %copy.48), calls=%async_computation | async-start | bytes 32768 | tf_op jit(solution)/shard_map/all_to_all | solution.py:50
  44.7 10.8 %all-gather.2 = s32[8,64,2]{1,2,0:T(2,128)S(1)} all-gather(s32[1,64,2]{1,2,0:T(2,128)S(1)} %bitcast.70), channel_id=1, replica_groups=mesh['dp'=32,'expert'=8] {'expert'}, dimensions={0}, use_global_device_ids=true | all-gather | bytes 4608 | tf_op jit(solution)/shard_map/all_gather | solution.py:58
  55.8 0.2 eq.47
  56.0 0.2 reshape.266
  56.2 9.0 %reduce-window.6 = s32[32,8,128]{2,1,0:T(8,128)S(1)} reduce-window(s32[32,8,128]{2,1,0:T(8,128)S(1)} %fusion.38, s32[]{:T(128)} %constant.99.clone.1), window={size=1x1x128 pad=0_0x0_0x127_0}, to_apply=%region_4.5 | reduce-window | flops 4161536 | bytes 262148 | tf_op jit(solution)/shard_map/reduce-window
  66.1 4.6 convolution_convert_fusion.1
  70.7 0.7 dynamic-slice
  72.1 0.7 reduce.3
  72.8 0.2 dynamic-update-slice
  73.0 6.7 %all-reduce = s32[256]{0:T(256)S(1)} all-reduce(s32[256]{0:T(256)S(1)} %dynamic-update-slice), channel_id=2, replica_groups=mesh['dp'=32,'expert'=8] {'expert'}, use_global_device_ids=true, to_apply=%add | all-reduce | flops 256 | bytes 2048 | tf_op jit(solution)/shard_map/all_gather | solution.py:57
  79.8 12.6 %all-gather.7.cloned.1.call-done = bf16[512,2048]{1,0:T(8,128)(2,1)} async-done(((bf16[64,2048]{1,0:T(8,128)(2,1)}), bf16[512,2048]{1,0:T(8,128)(2,1)}) %all-gather.7.cloned.1.call-update) | async-done | bytes 2097168 | tf_op jit(solution)/shard_map/all_gather | solution.py:55
  92.3 70.3 %all-reduce.3.cloned.1.call-done = bf16[256,2048]{1,0:T(8,128)(2,1)} async-done(((bf16[256,2048]{1,0:T(8,128)(2,1)}), bf16[256,2048]{1,0:T(8,128)(2,1)}) %all-reduce.3.cloned.1.call-update) | async-done | bytes 1048592 | tf_op jit(solution)/shard_map/psum | solution.py:62
  162.6 6.4 %scatter_fusion = bf16[512,2048]{1,0:T(8,128)(2,1)} fusion(bf16[512,2048]{1,0:T(8,128)(2,1)} %all-gather.7.cloned.1.call-done, s32[256]{0:T(256)S(1)} %compare_select_fusion.5, bf16[256,2048]{1,0:T(8,128)(2,1)} %all-reduce.3.cloned.1.call-done), kind=kCustom, calls=%fused_computation.4 | custom fusion | bytes 3146752 | tf_op jit(solution)/shard_map/scatter | solution.py:64
  169.1 2.2 fusion
  171.3 1.9 fusion.2
  173.2 22.1 %scatter_custom_fusion.1 = bf16[1536,2048]{1,0:T(8,128)(2,1)} fusion(s32[1024]{0:T(1024)S(1)} %get-tuple-element.14, bf16[512,2048]{1,0:T(8,128)(2,1)} %fusion.2, s32[1024]{0:T(1024)S(1)} %get-tuple-element.13, bf16[]{:T(256)} %constant.118.clone.1), kind=kCustom, calls=%fused_computation.13 | custom fusion | bytes 6291968
  195.3 146.9 %all_to_all.22 = bf16[32,48,2048]{2,1,0:T(8,128)(2,1)S(1)} all-to-all(bf16[32,48,2048]{2,1,0:T(8,128)(2,1)} %bitcast.61), channel_id=1, replica_groups=mesh['dp'=32,'expert'=8] {'dp'}, dimensions={0} | all-to-all | bytes 12582912 | tf_op jit(solution)/shard_map/all_to_all | solution.py:83
  342.2 2.7 copy-done.4
  344.9 3.0 fusion.13
  347.9 12.3 %convolution_convert_fusion = bf16[32,48,2048]{2,1,0:T(8,128)(2,1)} fusion(f32[32,48,176]{2,1,0:T(8,128)} %fusion.13, bf16[32,48,2048]{2,1,0:T(8,128)(2,1)} %copy-done.4, bf16[1,176,2048]{2,1,0:T(8,128)(2,1)S(1)} %copy-done.11, bf16[1,2048,176]{1,2,0:T(8,128)(2,1)S(1)} %copy-done.12), kind=kOutput, calls=%fused_computation.9 | convolution fusion | flops 2219360256 | bytes 15106048 | tf_op jit(solution)/shard_map/ncf,fd->ncd/dot_general | solution.py:87
  360.3 8.9 %copy.57 = bf16[32,48,2048]{2,0,1:T(8,128)(2,1)} copy(bf16[32,48,2048]{2,1,0:T(8,128)(2,1)} %convolution_convert_fusion) | data formatting | bytes 12582912 | tf_op jit(solution)/shard_map/convert_element_type | solution.py:91
  369.2 44.5 %reduce-scatter.3.cloned.1.call-done = bf16[32,6,2048]{2,0,1:T(8,128)(2,1)} async-done(((bf16[32,48,2048]{2,0,1:T(8,128)(2,1)}), bf16[32,6,2048]{2,0,1:T(8,128)(2,1)}) %reduce-scatter.3.cloned.1.call-update) | async-done | bytes 786448 | tf_op jit(solution)/shard_map/reduce_scatter | solution.py:90
  413.7 2.6 copy.58
  416.2 10.1 %all-to-all-start.3 = ((bf16[32,6,2048]{2,1,0:T(8,128)(2,1)}), bf16[32,6,2048]{2,1,0:T(8,128)(2,1)S(1)}, u32[]{:S(2)}, u32[]{:S(2)}) async-start(bf16[32,6,2048]{2,1,0:T(8,128)(2,1)} %copy.58), calls=%async_computation.4 | async-start | bytes 2097152 | tf_op jit(solution)/shard_map/all_to_all | solution.py:93
  426.4 0.3 reduce-scatter.5.cloned.1.call-start
  426.6 0.2 div.94
  426.9 0.3 and.78
  427.1 8.6 %all-gather.3 = s32[8,64,2]{1,2,0:T(2,128)S(1)} all-gather(s32[1,64,2]{1,2,0:T(2,128)S(1)} %bitcast.71), channel_id=1, replica_groups=mesh['dp'=32,'expert'=8] {'expert'}, dimensions={0}, use_global_device_ids=true | all-gather | bytes 4608 | tf_op jit(solution)/shard_map/all_gather | solution.py:59
  436.2 2.9 fusion.50
  439.1 13.1 %all-to-all-done.3 = bf16[32,6,2048]{2,1,0:T(8,128)(2,1)S(1)} async-done(((bf16[32,6,2048]{2,1,0:T(8,128)(2,1)}), bf16[32,6,2048]{2,1,0:T(8,128)(2,1)S(1)}, u32[]{:S(2)}, u32[]{:S(2)}) %all-to-all-start.3) | async-done | bytes 786464 | tf_op jit(solution)/shard_map/all_to_all | solution.py:93
  452.2 0.3 reshape.268
  452.4 6.1 %gather_fusion.2 = bf16[1024,2048]{1,0:T(8,128)(2,1)} fusion(bf16[192,2048]{1,0:T(8,128)(2,1)S(1)} %reshape.268, s32[1024]{0:T(1024)S(1)} %broadcast_clamp_fusion), kind=kCustom, calls=%fused_computation.3 | custom fusion | bytes 8392704 | tf_op jit(solution)/shard_map/gather | solution.py:96
  458.5 9.6 %reshape.273 = f32[512,2,2048]{2,1,0:T(2,128)} reshape(bf16[1024,2048]{1,0:T(8,128)(2,1)} %gather_fusion.2) | data formatting | bytes 12582912 | tf_op jit(solution)/shard_map/convert_element_type | solution.py:101
  468.2 15.5 %multiply_reduce_fusion = f32[512,2048]{1,0:T(8,128)} fusion(f32[512,2,2048]{2,1,0:T(2,128)} %reshape.273, f32[512,2]{1,0:T(8,128)S(1)} %fusion.31), kind=kLoop, calls=%fused_computation.6 | loop fusion | flops 3145728 | bytes 12587008 | tf_op jit(solution)/shard_map/reduce_sum | solution.py:100
  483.6 7.4 %add_convert_fusion = bf16[512,2048]{1,0:T(8,128)(2,1)} fusion(f32[512,2048]{1,0:T(8,128)} %multiply_reduce_fusion, bf16[352,2048]{1,0:T(8,128)(2,1)} %param.22, bf16[512,2048]{1,0:T(8,128)(2,1)} %fusion.2, bf16[2048,352]{0,1:T(8,128)(2,1)} %param.21, f32[512,352]{0,1:T(8,128)S(1)} %fusion.50), kind=kOutput, calls=%fused_computation.15 | convolution fusion | flops 1479573504 | bytes 11993088 | tf_op jit(solution)/shard_map/dot_general | solution.py:105
  491.1 34.4 %reduce-scatter.5.cloned.1.call-done = bf16[64,2048]{1,0:T(8,128)(2,1)} async-done(((bf16[512,2048]{1,0:T(8,128)(2,1)}), bf16[64,2048]{1,0:T(8,128)(2,1)}) %reduce-scatter.5.cloned.1.call-update) | async-done | bytes 262160 | tf_op jit(solution)/shard_map/reduce_scatter | solution.py:104
  525.5 1.8 add_convert_fusion.1
  (69 shorter events, 1.8 us)
Async XLA Ops:
  6.5 59.5 %copy-start = (bf16[4608,256]{1,0:T(8,128)(2,1)S(1)}, bf16[4608,256]{1,0:T(8,128)(2,1)}, u32[]{:S(2)}) copy-start(bf16[4608,256]{1,0:T(8,128)(2,1)} %param.17) | copy-start | bytes 7077892
  6.5 59.5 %all-gather.9.cloned.1.call-start = ((), (), s32[]{:S(2)}) async-start(), calls=%async_computation.10 | async-start | bytes 2654208 | tf_op jit(solution)/shard_map/all_gather | solution.py:56
  11.0 26.4 %copy-start.2 = (s32[32]{0:T(128)S(1)}, s32[32]{0:T(128)}, u32[]{:S(2)}) copy-start(s32[32]{0:T(128)} %param.16) | copy-start | bytes 388
  11.0 33.7 %copy-start.6 = (s32[64,2]{0,1:T(2,128)S(1)}, s32[64,2]{0,1:T(2,128)}, u32[]{:S(2)}) copy-start(s32[64,2]{0,1:T(2,128)} %param.26) | copy-start | bytes 1540
  35.8 30.0 %copy-start.9 = (s32[2]{0:T(128)S(1)}, s32[2]{0:T(128)}, u32[]{:S(2)}) copy-start(s32[2]{0:T(128)} %constant.129) | copy-start | bytes 28
  35.8 30.1 %copy-start.8 = (s32[2]{0:T(128)S(1)}, s32[2]{0:T(128)}, u32[]{:S(2)}) copy-start(s32[2]{0:T(128)} %constant.132) | copy-start | bytes 28
  36.6 55.7 %all-gather.7.cloned.1.call-start = ((), (), s32[]{:S(2)}) async-start(), calls=%async_computation.6 | async-start | bytes 2359296 | tf_op jit(solution)/shard_map/all_gather | solution.py:55
  38.8 33.3 %all-to-all-start = ((s32[32,1,1]{2,1,0:T(1,128)}), s32[32,1,1]{2,1,0:T(1,128)S(1)}, u32[]{:S(2)}, u32[]{:S(2)}) async-start(s32[32,1,1]{2,1,0:T(1,128)} %copy.48), calls=%async_computation | async-start | bytes 32768 | tf_op jit(solution)/shard_map/all_to_all | solution.py:50
  44.6 118.0 %all-reduce.3.cloned.1.call-start = ((), (), s32[]{:S(2)}) async-start(), calls=%async_computation.7 | async-start | bytes 2097152 | tf_op jit(solution)/shard_map/psum | solution.py:62
  66.0 4.7 copy-start.13
  70.7 343.0 %reduce-scatter.3.cloned.1.call-start = ((), (), s32[]{:S(2)}) async-start(), calls=%async_computation.8 | async-start | bytes 7077888 | tf_op jit(solution)/shard_map/reduce_scatter | solution.py:90
  79.8 91.6 %copy-start.5 = (f32[2048]{0:T(1024)S(1)}, f32[2048]{0:T(1024)}, u32[]{:S(2)}) copy-start(f32[2048]{0:T(1024)} %param.19) | copy-start | bytes 24580
  169.1 2.3 copy-start.3
  195.3 149.6 %copy-start.10 = (bf16[1,2048,176]{1,2,0:T(8,128)(2,1)S(1)}, bf16[1,2048,176]{1,2,0:T(8,128)(2,1)}, u32[]{:S(2)}) copy-start(bf16[1,2048,176]{1,2,0:T(8,128)(2,1)} %param.23) | copy-start | bytes 2162692
  342.2 2.7 copy-start.4
  344.9 3.0 copy-start.11
  344.9 3.0 copy-start.12
  369.2 58.0 %copy-start.7 = (s32[64,2]{0,1:T(2,128)S(1)}, s32[64,2]{0,1:T(2,128)}, u32[]{:S(2)}) copy-start(s32[64,2]{0,1:T(2,128)} %param.27) | copy-start | bytes 1540
  416.2 35.9 %all-to-all-start.3 = ((bf16[32,6,2048]{2,1,0:T(8,128)(2,1)}), bf16[32,6,2048]{2,1,0:T(8,128)(2,1)S(1)}, u32[]{:S(2)}, u32[]{:S(2)}) async-start(bf16[32,6,2048]{2,1,0:T(8,128)(2,1)} %copy.58), calls=%async_computation.4 | async-start | bytes 2097152 | tf_op jit(solution)/shard_map/all_to_all | solution.py:93
  426.4 99.1 %reduce-scatter.5.cloned.1.call-start = ((), (), s32[]{:S(2)}) async-start(), calls=%async_computation.9 | async-start | bytes 2359296 | tf_op jit(solution)/shard_map/reduce_scatter | solution.py:104
  483.6 43.7 %copy-start.1 = (bf16[4608,256]{1,0:T(8,128)(2,1)S(1)}, bf16[4608,256]{1,0:T(8,128)(2,1)}, u32[]{:S(2)}) copy-start(bf16[4608,256]{1,0:T(8,128)(2,1)} %param.17) | copy-start | bytes 7077892
Sparse Core Ops, SparseCore 0:
  36.8 25.3 all-gather.8
  64.0 28.2 all-gather.6
  94.7 67.9 all-reduce.2
  369.3 44.3 reduce-scatter.2
  491.2 34.2 reduce-scatter.4
where the time goes:
time: 541 us; the launch traced here: 534 us
  blocking collectives  196 us (36%)
  waiting for transfers between devices  176 us (33%)
  local copies, waits for them, and re-layouts  66.2 us (12%)
  other arithmetic  35 us (6%)
  matrix products  30.3 us (6%)
  starting transfers between devices  16.3 us (3%)
  between operations  14.5 us (3%)
    all_to_all x1, blocking collectives, shards(): slots = lax.all_to_all(send, 'dp', split_axis=0, concat_axis=0, tiled=True)  147 us
    psum x1, waiting for transfers between devices, shards(): projected = lax.psum(partial_value.astype(jnp.bfloat16), 'expert')  70.3 us
    reduce_scatter x1, waiting for transfers between devices, shards(): lax.psum_scatter(partial_out.astype(jnp.bfloat16), 'expert', scatter_dime...  44.5 us
    reduce_scatter x1, waiting for transfers between devices, shards(): lax.psum_scatter((jnp.dot(shared_hidden, shared_down, preferred_element_t...  34.4 us
    unnamed x34, local copies, waits for them, and re-layouts  26 us
    all_to_all x1, blocking collectives, shards(): lax.all_to_all(sorted_feats, 'dp', split_axis=0, concat_axis=0, tiled=True)  23.1 us
    reduce_sum x1, other arithmetic, shards(): jnp.sum((picked.astype(jnp.float32) * coef[:, None]).reshape(group_rows,...  15.5 us
    all_to_all x1, waiting for transfers between devices, shards(): lax.all_to_all(summed, 'dp', split_axis=0, concat_axis=0, tiled=True)  13.1 us
  transfers between devices with their start and end apart: 7, of which 5 were waited for; matrix products, arithmetic and copies ran while one was open for 4% of the time, Pallas kernels for 0%

commit v1 on v0

--- a/solution.py
+++ b/solution.py
@@ -59,7 +59,7 @@
         lax.all_gather(route_wts, "expert", axis=0, tiled=True),
     )
     partial_value = project_part(feats, proj_in, proj_out)
-    projected = lax.psum(partial_value.astype(jnp.bfloat16), "expert")
+    projected = jnp.sum(lax.all_gather(partial_value.astype(jnp.bfloat16), "expert"), axis=0)
     block_start = jnp.arange(offsets.shape[0], dtype=jnp.int32) // img_dev * tok_dev
     embed_group = texts.at[offsets + block_start].set(projected)
     normed = normalize(embed_group, norm_gain)

time: 541 us -> 530 us (0.980)
  waiting for transfers between devices: 176 us -> 153 us
    psum x1 -> x0, waiting for transfers between devices: 70.3 us -> none  [shards(): projected = lax.psum(partial_value.astype(jnp.bfloat16), 'expert')]
    all_gather x1, waiting for transfers between devices: 0.02 us -> 25.4 us  [shards(): lax.all_gather(moved_feats, 'expert', axis=0, tiled=True)]
    all_gather x1, waiting for transfers between devices: 12.6 us -> 24.7 us  [shards(): lax.all_gather(text_embed, 'expert', axis=0, tiled=True)]
    all_gather x0 -> x1, waiting for transfers between devices: none -> 11.6 us  [shards(): lax.all_gather(partial_value.astype(jnp.bfloat16), 'expert')]
  transfers between devices with their start and end apart: 7 -> 7, of which waited for: 5 -> 6; matrix products, arithmetic and copies ran while one was open for 4% -> 4% of each run, Pallas kernels for 0% -> 0%
where the time goes in v1:
time: 530 us; the launch traced here: 521 us
  blocking collectives  197 us (37%)
  waiting for transfers between devices  153 us (29%)
  local copies, waits for them, and re-layouts  65.4 us (12%)
  other arithmetic  40.2 us (8%)
  matrix products  30.4 us (6%)
  starting transfers between devices  20.7 us (4%)
  between operations  14.4 us (3%)
    all_to_all x1, blocking collectives, shards(): slots = lax.all_to_all(send, 'dp', split_axis=0, concat_axis=0, tiled=True)  149 us
    reduce_scatter x1, waiting for transfers between devices, shards(): lax.psum_scatter(partial_out.astype(jnp.bfloat16), 'expert', scatter_dime...  42.9 us
    reduce_scatter x1, waiting for transfers between devices, shards(): lax.psum_scatter((jnp.dot(shared_hidden, shared_down, preferred_element_t...  34.4 us
    unnamed x34, local copies, waits for them, and re-layouts  26 us
    all_gather x1, waiting for transfers between devices, shards(): lax.all_gather(moved_feats, 'expert', axis=0, tiled=True)  25.4 us
    all_gather x1, waiting for transfers between devices, shards(): lax.all_gather(text_embed, 'expert', axis=0, tiled=True)  24.7 us
    all_to_all x1, blocking collectives, shards(): lax.all_to_all(sorted_feats, 'dp', split_axis=0, concat_axis=0, tiled=True)  23.1 us
    reduce_sum x1, other arithmetic, shards(): jnp.sum((picked.astype(jnp.float32) * coef[:, None]).reshape(group_rows,...  15.5 us
  transfers between devices with their start and end apart: 7, of which 6 were waited for; matrix products, arithmetic and copies ran while one was open for 4% of the time, Pallas kernels for 0%

profile of v1, /device:TPU:2, one launch (start us, length us, event | category | flops | bytes accessed | tf_op | source)
XLA Modules:
  0.0 521.3 jit_solution(7797983607405214158)
XLA Ops:
  6.5 0.8 and_select_fusion.4
  7.4 1.6 sort.17
  9.0 2.0 gather_fusion.1
  11.0 0.5 broadcast.394
  11.5 0.8 reduce.8
  12.4 23.1 %all_to_all.21 = bf16[32,2,2304]{2,1,0:T(2,128)(2,1)S(1)} all-to-all(bf16[32,2,2304]{2,1,0:T(2,128)(2,1)S(1)} %reshape.351), channel_id=1, replica_groups=mesh['dp'=32,'expert'=8] {'dp'}, dimensions={0} | all-to-all | bytes 589824 | tf_op jit(solution)/shard_map/all_to_all | solution.py:49
  35.5 0.2 reshape.352
  35.8 0.8 copy.50
  36.7 25.4 %all-gather.11.cloned.1.call-done = bf16[256,1,4608]{2,0,1:T(8,128)(2,1)} async-done(((bf16[32,1,4608]{2,0,1:T(8,128)(2,1)}), bf16[256,1,4608]{2,0,1:T(8,128)(2,1)}) %all-gather.11.cloned.1.call-update) | async-done | bytes 2359312 | tf_op jit(solution)/shard_map/all_gather | solution.py:56
  62.1 4.7 convolution_convert_fusion.1
  66.8 0.7 all-gather.9.cloned.1.call-update
  67.5 0.7 gather_fusion
  68.2 0.7 copy.48
  68.9 10.1 %all-to-all-start = ((s32[32,1,1]{2,1,0:T(1,128)}), s32[32,1,1]{2,1,0:T(1,128)S(1)}, u32[]{:S(2)}, u32[]{:S(2)}) async-start(s32[32,1,1]{2,1,0:T(1,128)} %copy.48), calls=%async_computation | async-start | bytes 32768 | tf_op jit(solution)/shard_map/all_to_all | solution.py:50
  79.1 9.4 %all-gather.3 = s32[8,64,2]{1,2,0:T(2,128)S(1)} all-gather(s32[1,64,2]{1,2,0:T(2,128)S(1)} %bitcast.72), channel_id=1, replica_groups=mesh['dp'=32,'expert'=8] {'expert'}, dimensions={0}, use_global_device_ids=true | all-gather | bytes 4608 | tf_op jit(solution)/shard_map/all_gather | solution.py:58
  89.3 9.0 %reduce-window.6 = s32[32,8,128]{2,1,0:T(8,128)S(1)} reduce-window(s32[32,8,128]{2,1,0:T(8,128)S(1)} %fusion.38, s32[]{:T(128)} %constant.100.clone.1), window={size=1x1x128 pad=0_0x0_0x127_0}, to_apply=%region_4.5 | reduce-window | flops 4161536 | bytes 262148 | tf_op jit(solution)/shard_map/reduce-window
  99.1 0.6 dynamic-slice
  100.4 0.7 reduce.4
  101.1 0.2 dynamic-update-slice
  101.3 7.0 %all-reduce = s32[256]{0:T(256)S(1)} all-reduce(s32[256]{0:T(256)S(1)} %dynamic-update-slice), channel_id=2, replica_groups=mesh['dp'=32,'expert'=8] {'expert'}, use_global_device_ids=true, to_apply=%add | all-reduce | flops 256 | bytes 2048 | tf_op jit(solution)/shard_map/all_gather | solution.py:57
  108.3 11.6 %all-gather.13.cloned.1.call-done = bf16[2048,2048]{1,0:T(8,128)(2,1)} async-done(((bf16[256,2048]{1,0:T(8,128)(2,1)}), bf16[2048,2048]{1,0:T(8,128)(2,1)}) %all-gather.13.cloned.1.call-update) | async-done | bytes 8388624 | tf_op jit(solution)/shard_map/all_gather | solution.py:62
  119.9 5.2 reduce_sum.48
  125.1 24.7 %all-gather.9.cloned.1.call-done = bf16[512,2048]{1,0:T(8,128)(2,1)} async-done(((bf16[64,2048]{1,0:T(8,128)(2,1)}), bf16[512,2048]{1,0:T(8,128)(2,1)}) %all-gather.9.cloned.1.call-update) | async-done | bytes 2097168 | tf_op jit(solution)/shard_map/all_gather | solution.py:55
  149.8 5.8 %scatter_fusion = bf16[512,2048]{1,0:T(8,128)(2,1)} fusion(bf16[512,2048]{1,0:T(8,128)(2,1)} %all-gather.9.cloned.1.call-done, s32[256]{0:T(256)S(1)} %compare_select_fusion.5, bf16[256,2048]{1,0:T(8,128)(2,1)S(1)} %reduce_sum.48), kind=kCustom, calls=%fused_computation.4 | custom fusion | bytes 3146752 | tf_op jit(solution)/shard_map/scatter | solution.py:64
  155.5 2.2 fusion
  157.8 1.9 fusion.2
  159.7 22.1 %scatter_custom_fusion.1 = bf16[1536,2048]{1,0:T(8,128)(2,1)} fusion(s32[1024]{0:T(1024)S(1)} %get-tuple-element.14, bf16[512,2048]{1,0:T(8,128)(2,1)} %fusion.2, s32[1024]{0:T(1024)S(1)} %get-tuple-element.13, bf16[]{:T(256)} %constant.115.clone.1), kind=kCustom, calls=%fused_computation.13 | custom fusion | bytes 6291968
  181.8 149.3 %all_to_all.22 = bf16[32,48,2048]{2,1,0:T(8,128)(2,1)S(1)} all-to-all(bf16[32,48,2048]{2,1,0:T(8,128)(2,1)} %bitcast.62), channel_id=1, replica_groups=mesh['dp'=32,'expert'=8] {'dp'}, dimensions={0} | all-to-all | bytes 12582912 | tf_op jit(solution)/shard_map/all_to_all | solution.py:83
  331.1 2.7 copy-done.4
  333.7 3.0 fusion.13
  336.8 12.3 %convolution_convert_fusion = bf16[32,48,2048]{2,1,0:T(8,128)(2,1)} fusion(f32[32,48,176]{2,1,0:T(8,128)} %fusion.13, bf16[32,48,2048]{2,1,0:T(8,128)(2,1)} %copy-done.4, bf16[1,176,2048]{2,1,0:T(8,128)(2,1)S(1)} %copy-done.11, bf16[1,2048,176]{1,2,0:T(8,128)(2,1)S(1)} %copy-done.12), kind=kOutput, calls=%fused_computation.9 | convolution fusion | flops 2219360256 | bytes 15106048 | tf_op jit(solution)/shard_map/ncf,fd->ncd/dot_general | solution.py:87
  349.1 8.9 %copy.57 = bf16[32,48,2048]{2,0,1:T(8,128)(2,1)} copy(bf16[32,48,2048]{2,1,0:T(8,128)(2,1)} %convolution_convert_fusion) | data formatting | bytes 12582912 | tf_op jit(solution)/shard_map/convert_element_type | solution.py:91
  358.0 42.9 %reduce-scatter.3.cloned.1.call-done = bf16[32,6,2048]{2,0,1:T(8,128)(2,1)} async-done(((bf16[32,48,2048]{2,0,1:T(8,128)(2,1)}), bf16[32,6,2048]{2,0,1:T(8,128)(2,1)}) %reduce-scatter.3.cloned.1.call-update) | async-done | bytes 786448 | tf_op jit(solution)/shard_map/reduce_scatter | solution.py:90
  400.9 2.6 copy.58
  403.5 10.2 %all-to-all-start.3 = ((bf16[32,6,2048]{2,1,0:T(8,128)(2,1)}), bf16[32,6,2048]{2,1,0:T(8,128)(2,1)S(1)}, u32[]{:S(2)}, u32[]{:S(2)}) async-start(bf16[32,6,2048]{2,1,0:T(8,128)(2,1)} %copy.58), calls=%async_computation.4 | async-start | bytes 2097152 | tf_op jit(solution)/shard_map/all_to_all | solution.py:93
  413.7 0.3 reduce-scatter.5.cloned.1.call-start
  413.9 0.2 div.94
  414.1 0.3 and.78
  414.4 8.6 %all-gather.4 = s32[8,64,2]{1,2,0:T(2,128)S(1)} all-gather(s32[1,64,2]{1,2,0:T(2,128)S(1)} %bitcast.73), channel_id=1, replica_groups=mesh['dp'=32,'expert'=8] {'expert'}, dimensions={0}, use_global_device_ids=true | all-gather | bytes 4608 | tf_op jit(solution)/shard_map/all_gather | solution.py:59
  423.5 2.9 fusion.50
  426.4 13.1 %all-to-all-done.3 = bf16[32,6,2048]{2,1,0:T(8,128)(2,1)S(1)} async-done(((bf16[32,6,2048]{2,1,0:T(8,128)(2,1)}), bf16[32,6,2048]{2,1,0:T(8,128)(2,1)S(1)}, u32[]{:S(2)}, u32[]{:S(2)}) %all-to-all-start.3) | async-done | bytes 786464 | tf_op jit(solution)/shard_map/all_to_all | solution.py:93
  439.5 0.3 reshape.268
  439.7 6.1 %gather_fusion.2 = bf16[1024,2048]{1,0:T(8,128)(2,1)} fusion(bf16[192,2048]{1,0:T(8,128)(2,1)S(1)} %reshape.268, s32[1024]{0:T(1024)S(1)} %broadcast_clamp_fusion), kind=kCustom, calls=%fused_computation.3 | custom fusion | bytes 8392704 | tf_op jit(solution)/shard_map/gather | solution.py:96
  445.8 9.6 %reshape.273 = f32[512,2,2048]{2,1,0:T(2,128)} reshape(bf16[1024,2048]{1,0:T(8,128)(2,1)} %gather_fusion.2) | data formatting | bytes 12582912 | tf_op jit(solution)/shard_map/convert_element_type | solution.py:101
  455.5 15.5 %multiply_reduce_fusion = f32[512,2048]{1,0:T(8,128)} fusion(f32[512,2,2048]{2,1,0:T(2,128)} %reshape.273, f32[512,2]{1,0:T(8,128)S(1)} %fusion.31), kind=kLoop, calls=%fused_computation.6 | loop fusion | flops 3145728 | bytes 12587008 | tf_op jit(solution)/shard_map/reduce_sum | solution.py:100
  470.9 7.4 %add_convert_fusion = bf16[512,2048]{1,0:T(8,128)(2,1)} fusion(f32[512,2048]{1,0:T(8,128)} %multiply_reduce_fusion, bf16[352,2048]{1,0:T(8,128)(2,1)} %param.22, bf16[512,2048]{1,0:T(8,128)(2,1)} %fusion.2, bf16[2048,352]{0,1:T(8,128)(2,1)} %param.21, f32[512,352]{0,1:T(8,128)S(1)} %fusion.50), kind=kOutput, calls=%fused_computation.15 | convolution fusion | flops 1479573504 | bytes 11993088 | tf_op jit(solution)/shard_map/dot_general | solution.py:105
  478.4 34.4 %reduce-scatter.5.cloned.1.call-done = bf16[64,2048]{1,0:T(8,128)(2,1)} async-done(((bf16[512,2048]{1,0:T(8,128)(2,1)}), bf16[64,2048]{1,0:T(8,128)(2,1)}) %reduce-scatter.5.cloned.1.call-update) | async-done | bytes 262160 | tf_op jit(solution)/shard_map/reduce_scatter | solution.py:104
  512.7 1.8 add_convert_fusion.1
  (70 shorter events, 2.2 us)
Async XLA Ops:
  6.5 55.5 %copy-start = (bf16[4608,256]{1,0:T(8,128)(2,1)S(1)}, bf16[4608,256]{1,0:T(8,128)(2,1)}, u32[]{:S(2)}) copy-start(bf16[4608,256]{1,0:T(8,128)(2,1)} %param.17) | copy-start | bytes 7077892
  6.5 55.5 %all-gather.11.cloned.1.call-start = ((), (), s32[]{:S(2)}) async-start(), calls=%async_computation.9 | async-start | bytes 2654208 | tf_op jit(solution)/shard_map/all_gather | solution.py:56
  36.6 30.9 %copy-start.2 = (s32[32]{0:T(128)S(1)}, s32[32]{0:T(128)}, u32[]{:S(2)}) copy-start(s32[32]{0:T(128)} %param.16) | copy-start | bytes 388
  36.6 42.5 %copy-start.6 = (s32[64,2]{0,1:T(2,128)S(1)}, s32[64,2]{0,1:T(2,128)}, u32[]{:S(2)}) copy-start(s32[64,2]{0,1:T(2,128)} %param.26) | copy-start | bytes 1540
  36.6 83.3 %all-gather.13.cloned.1.call-start = ((), (), s32[]{:S(2)}) async-start(), calls=%async_computation.10 | async-start | bytes 9437184 | tf_op jit(solution)/shard_map/all_gather | solution.py:62
  66.7 32.2 %copy-start.9 = (s32[2]{0:T(128)S(1)}, s32[2]{0:T(128)}, u32[]{:S(2)}) copy-start(s32[2]{0:T(128)} %constant.130) | copy-start | bytes 28
  66.7 32.3 %copy-start.8 = (s32[2]{0:T(128)S(1)}, s32[2]{0:T(128)}, u32[]{:S(2)}) copy-start(s32[2]{0:T(128)} %constant.133) | copy-start | bytes 28
  66.8 32.4 %copy-start.13 = (u32[256]{0:T(256)S(1)}, u32[256]{0:T(256)}, u32[]{:S(2)}) copy-start(u32[256]{0:T(256)} %constant.140) | copy-start | bytes 3076
  66.8 83.0 %all-gather.9.cloned.1.call-start = ((), (), s32[]{:S(2)}) async-start(), calls=%async_computation.6 | async-start | bytes 2359296 | tf_op jit(solution)/shard_map/all_gather | solution.py:55
  68.9 31.5 %all-to-all-start = ((s32[32,1,1]{2,1,0:T(1,128)}), s32[32,1,1]{2,1,0:T(1,128)S(1)}, u32[]{:S(2)}, u32[]{:S(2)}) async-start(s32[32,1,1]{2,1,0:T(1,128)} %copy.48), calls=%async_computation | async-start | bytes 32768 | tf_op jit(solution)/shard_map/all_to_all | solution.py:50
  79.1 321.8 %reduce-scatter.3.cloned.1.call-start = ((), (), s32[]{:S(2)}) async-start(), calls=%async_computation.7 | async-start | bytes 7077888 | tf_op jit(solution)/shard_map/reduce_scatter | solution.py:90
  125.1 32.7 %copy-start.5 = (f32[2048]{0:T(1024)S(1)}, f32[2048]{0:T(1024)}, u32[]{:S(2)}) copy-start(f32[2048]{0:T(1024)} %param.19) | copy-start | bytes 24580
  155.5 2.3 copy-start.3
  181.8 152.0 %copy-start.10 = (bf16[1,2048,176]{1,2,0:T(8,128)(2,1)S(1)}, bf16[1,2048,176]{1,2,0:T(8,128)(2,1)}, u32[]{:S(2)}) copy-start(bf16[1,2048,176]{1,2,0:T(8,128)(2,1)} %param.23) | copy-start | bytes 2162692
  331.1 2.7 copy-start.4
  333.7 3.0 copy-start.11
  333.7 3.0 copy-start.12
  358.0 56.4 %copy-start.7 = (s32[64,2]{0,1:T(2,128)S(1)}, s32[64,2]{0,1:T(2,128)}, u32[]{:S(2)}) copy-start(s32[64,2]{0,1:T(2,128)} %param.27) | copy-start | bytes 1540
  403.5 36.0 %all-to-all-start.3 = ((bf16[32,6,2048]{2,1,0:T(8,128)(2,1)}), bf16[32,6,2048]{2,1,0:T(8,128)(2,1)S(1)}, u32[]{:S(2)}, u32[]{:S(2)}) async-start(bf16[32,6,2048]{2,1,0:T(8,128)(2,1)} %copy.58), calls=%async_computation.4 | async-start | bytes 2097152 | tf_op jit(solution)/shard_map/all_to_all | solution.py:93
  413.7 99.1 %reduce-scatter.5.cloned.1.call-start = ((), (), s32[]{:S(2)}) async-start(), calls=%async_computation.8 | async-start | bytes 2359296 | tf_op jit(solution)/shard_map/reduce_scatter | solution.py:104
  470.9 43.6 %copy-start.1 = (bf16[4608,256]{1,0:T(8,128)(2,1)S(1)}, bf16[4608,256]{1,0:T(8,128)(2,1)}, u32[]{:S(2)}) copy-start(bf16[4608,256]{1,0:T(8,128)(2,1)} %param.17) | copy-start | bytes 7077892
Sparse Core Ops, SparseCore 0:
  36.7 25.3 all-gather.10
  66.9 52.9 all-gather.12
  121.8 27.9 all-gather.8
  358.1 42.7 reduce-scatter.2
  478.5 34.1 reduce-scatter.4
